TPU v7x, 256 devices: a whole 4x4x8 slice. The times are simulated.
256 devices in a mesh: narrow: 16 (over z, core), wide: 16 (over x, y).
Axes of the slice: x: 4, y: 4, z: 8, core: 2. Of those that a mesh axis runs over, the one named last changes fastest.
Arguments:
- inputs: bfloat16 [2048, 8192], P('narrow', 'wide'), may hold values from -6 to 6
- gate_blocks: bfloat16 [112, 16, 128, 128], P('wide', 'narrow'), may hold values from -0.125 to 0.125
- up_blocks: bfloat16 [112, 16, 128, 128], P('wide', 'narrow'), may hold values from -0.125 to 0.125
- pattern: int32 [112, 16], P('wide'), may hold values from 0 to 63, as said below
- grad_hidden: bfloat16 [2048, 14336], P('narrow', 'wide'), may hold values from -0.59765625 to 0.59765625
Outputs:
- hidden: bfloat16 [2048, 14336], P('narrow', 'wide')
- grad_inputs: bfloat16 [2048, 8192], P('narrow', 'wide')
- grad_gate: bfloat16 [112, 16, 128, 128], P('wide', 'narrow')
- grad_up: bfloat16 [112, 16, 128, 128], P('wide', 'narrow')
Inputs may be any that keep to these rules, and one draw needn't show every extreme that they name: pattern[j, k] = b_j XOR m_k, with one offset b_j for each block column and 16 distinct masks m_k common to all block columns, so each block column lists 16 distinct block rows.
All inputs are finite; a program needn't handle non-finite values.
Results may differ from a plain program's by a relative error of at most 0.023.
Values may be sent and summed in bfloat16 or wider, within the bound.
A program may use at most 128 MiB of HBM per device.

v0:
```python
import jax
import jax.numpy as jnp
from jax import lax
from jax.sharding import PartitionSpec as P


def silu_parts(gate_sum):
    sigmoid_value = jax.nn.sigmoid(gate_sum)
    return (gate_sum * sigmoid_value, sigmoid_value * (1.0 + gate_sum * (1.0 - sigmoid_value)))


def shards(inputs, gate_blocks, up_blocks, pattern, grad_hidden):
    tokens_here = inputs.shape[0]
    block_size = gate_blocks.shape[2]
    columns = gate_blocks.shape[0]
    full_inputs = lax.all_gather(inputs, "wide", axis=1, tiled=True)
    row_blocks = full_inputs.shape[1] // block_size
    input_blocks = full_inputs.reshape(tokens_here, row_blocks, block_size)

    def picks_for():
        return jnp.take(input_blocks, pattern, axis=1)

    gate_all, up_all = (
        lax.all_gather(gate_blocks, "narrow", axis=1, tiled=True),
        lax.all_gather(up_blocks, "narrow", axis=1, tiled=True),
    )
    pieces = (gate_all, up_all)
    picked = picks_for()
    gate_sum = jnp.einsum("tjkb,jkbc->tjc", picked, pieces[0], preferred_element_type=jnp.float32)
    up_sum = jnp.einsum("tjkb,jkbc->tjc", picked, pieces[1], preferred_element_type=jnp.float32)
    gate_sum, up_sum = (gate_sum, up_sum)
    activation, derivative = silu_parts(gate_sum)
    hidden = (activation * up_sum).astype(jnp.bfloat16)
    cotangent = grad_hidden.reshape(tokens_here, columns, block_size).astype(jnp.float32)
    d_gate = (cotangent * up_sum * derivative).astype(jnp.bfloat16)
    d_up = (cotangent * activation).astype(jnp.bfloat16)
    zero_inputs = jnp.zeros((tokens_here, row_blocks, block_size), jnp.float32)
    pieces = (gate_all, up_all)
    number_slots = pieces[0].shape[1]

    def one_slot(k, running):
        gate_slot = lax.dynamic_index_in_dim(pieces[0], k, 1, keepdims=False)
        up_slot = lax.dynamic_index_in_dim(pieces[1], k, 1, keepdims=False)
        contribution = jnp.einsum(
            "tjc,jbc->tjb", d_gate, gate_slot, preferred_element_type=jnp.float32
        )
        contribution = contribution + jnp.einsum(
            "tjc,jbc->tjb", d_up, up_slot, preferred_element_type=jnp.float32
        )
        targets = lax.dynamic_index_in_dim(pattern, k, 1, keepdims=False)
        return running.at[:, targets].add(contribution)

    partial_inputs = lax.fori_loop(0, number_slots, one_slot, zero_inputs)
    grad_inputs = lax.psum_scatter(
        partial_inputs.reshape(tokens_here, row_blocks * block_size).astype(jnp.bfloat16),
        "wide",
        scatter_dimension=1,
        tiled=True,
    )
    picked_all = picks_for()
    gate_terms = jnp.einsum(
        "tjkb,tjc->jkbc", picked_all, d_gate, preferred_element_type=jnp.float32
    )
    up_terms = jnp.einsum("tjkb,tjc->jkbc", picked_all, d_up, preferred_element_type=jnp.float32)
    grad_gate, grad_up = (
        lax.psum_scatter(
            gate_terms.astype(jnp.bfloat16), "narrow", scatter_dimension=1, tiled=True
        ).astype(jnp.float32),
        lax.psum_scatter(
            up_terms.astype(jnp.bfloat16), "narrow", scatter_dimension=1, tiled=True
        ).astype(jnp.float32),
    )
    return (
        hidden.reshape(tokens_here, columns * block_size),
        grad_inputs,
        grad_gate.astype(jnp.bfloat16),
        grad_up.astype(jnp.bfloat16),
    )


def solution(mesh):
    placed = (
        P("narrow", "wide"),
        P("wide", "narrow", None, None),
        P("wide", "narrow", None, None),
        P("wide", None),
        P("narrow", "wide"),
    )
    return jax.shard_map(
        shards,
        mesh=mesh,
        in_specs=placed,
        out_specs=(
            P("narrow", "wide"),
            P("narrow", "wide"),
            P("wide", "narrow", None, None),
            P("wide", "narrow", None, None),
        ),
        check_vma=False,
    )
```

profile of v0, /device:TPU:28, one launch (start us, length us, event | category | flops | bytes accessed | tf_op | source)
XLA Modules:
  0.0 383.0 jit_solution(9591232748475014344)
XLA Ops:
  7.2 1.7 copy.60
  8.9 1.8 copy.65
  10.8 1.8 copy.63
  16.0 45.8 %all-gather.4.cloned.1.call-done = bf16[128,8192]{0,1:T(8,128)(2,1)} async-done(((bf16[128,512]{0,1:T(8,128)(2,1)}), bf16[128,8192]{0,1:T(8,128)(2,1)}) %all-gather.4.cloned.1.call-update) | async-done | bytes 2097168 | tf_op jit(solution)/shard_map/all_gather | solution.py:16
  61.8 3.2 copy.61
  65.0 3.0 gather_fusion
  67.9 6.1 %copy.62 = bf16[7,16,128,128]{2,3,1,0:T(8,128)(2,1)} copy(bf16[7,16,128,128]{3,2,1,0:T(8,128)(2,1)} %bitcast.89) | data formatting | bytes 7340032 | tf_op jit(solution)/shard_map/jit(_take)/gather | solution.py:21
  74.0 33.1 %all-gather.8.cloned.1.call-done = bf16[7,16,128,128]{2,3,1,0:T(8,128)(2,1)} async-done(((bf16[7,1,128,128]{2,3,1,0:T(8,128)(2,1)}), bf16[7,16,128,128]{2,3,1,0:T(8,128)(2,1)}) %all-gather.8.cloned.1.call-update) | async-done | bytes 3670032 | tf_op jit(solution)/shard_map/all_gather | solution.py:25
  107.1 4.4 %fusion.27 = f32[128,7,128]{0,2,1:T(8,128)S(1)} fusion(bf16[7,16,128,128]{2,3,1,0:T(8,128)(2,1)} %all-gather.8.cloned.1.call-done, bf16[7,16,128,128]{2,3,1,0:T(8,128)(2,1)} %copy.62, pred[7,16]{1,0:T(8,128)(4,1)S(1)} %compare_and_fusion), kind=kOutput, calls=%fused_computation.31 | convolution fusion | flops 471597056 | bytes 7798896 | tf_op jit(solution)/shard_map/tjkb,jkbc->tjc/dot_general | solution.py:30
  111.5 38.3 %all-gather.6.cloned.1.call-done = bf16[7,16,128,128]{2,3,1,0:T(8,128)(2,1)} async-done(((bf16[7,1,128,128]{2,3,1,0:T(8,128)(2,1)}), bf16[7,16,128,128]{2,3,1,0:T(8,128)(2,1)}) %all-gather.6.cloned.1.call-update) | async-done | bytes 3670032 | tf_op jit(solution)/shard_map/all_gather | solution.py:24
  149.8 4.5 %multiply_convert_fusion = (bf16[128,7,128]{0,2,1:T(8,128)(2,1)S(1)}, bf16[128,7,128]{0,2,1:T(8,128)(2,1)S(1)}, bf16[128,7,128]{0,2,1:T(8,128)(2,1)S(1)}) fusion(f32[128,7,128]{0,2,1:T(8,128)S(1)} %bitcast.91, f32[128,7,128]{0,2,1:T(8,128)S(1)} %fusion.27, bf16[7,16,128,128]{2,3,1,0:T(8,128)(2,1)} %all-gather.6.cloned.1.call-done, ...), kind=kOutput, calls=%fused_computation.33 | convolution fusion | flops 473317376 | bytes 8945776 | tf_op jit(solution)/shard_map/tjkb,jkbc->tjc/dot_general | solution.py:29
  154.5 5.1 %fusion.17 = bf16[7,16,128,128]{3,2,1,0:T(8,128)(2,1)} fusion(bf16[7,16,128,128]{2,3,1,0:T(8,128)(2,1)} %copy.62, pred[7,16]{1,0:T(8,128)(4,1)S(1)} %compare_and_fusion, bf16[128,7,128]{0,2,1:T(8,128)(2,1)S(1)} %get-tuple-element.191), kind=kOutput, calls=%fused_computation.23 | convolution fusion | flops 473432064 | bytes 7569520 | tf_op jit(solution)/shard_map/tjkb,tjc->jkbc/dot_general | solution.py:61
  159.8 5.0 %fusion.20 = bf16[7,16,128,128]{3,2,1,0:T(8,128)(2,1)} fusion(bf16[7,16,128,128]{2,3,1,0:T(8,128)(2,1)} %copy.62, pred[7,16]{1,0:T(8,128)(4,1)S(1)} %compare_and_fusion, bf16[128,7,128]{0,2,1:T(8,128)(2,1)S(1)} %get-tuple-element.190), kind=kOutput, calls=%fused_computation.24 | convolution fusion | flops 473432064 | bytes 7569520 | tf_op jit(solution)/shard_map/tjkb,tjc->jkbc/dot_general | solution.py:64
  164.9 2.5 broadcast_in_dim.15
  167.4 85.9 %while.13 = (s32[]{:T(128)}, f32[128,64,128]{2,0,1:T(8,128)}, s32[7,16]{0,1:T(8,128)S(1)}, bf16[7,16,128,128]{2,3,1,0:T(8,128)(2,1)}, bf16[128,7,128]{2,0,1:T(8,...) while((s32[]{:T(128)}, f32[128,64,128]{2,0,1:T(8,128)}, ...), condition=%wide.region_2.4_spmd, body=%wide.region_0.3_spmd.sunk | while | flops 58949656 | bytes 4587709 | solution.py:53
  168.6 1.3 fusion.57
  170.1 2.6 scatter_fusion
  173.9 1.3 fusion.57
  175.4 2.6 scatter_fusion
  178.1 1.2 fusion.56
  179.3 1.3 fusion.57
  180.8 2.7 scatter_fusion
  183.5 1.3 fusion.56
  184.7 1.3 fusion.57
  186.2 2.7 scatter_fusion
  188.8 1.3 fusion.56
  190.1 1.3 fusion.57
  191.5 2.6 scatter_fusion
  194.2 1.2 fusion.56
  195.4 1.3 fusion.57
  196.9 2.6 scatter_fusion
  199.5 1.2 fusion.56
  200.8 1.3 fusion.57
  202.2 2.7 scatter_fusion
  204.9 1.3 fusion.56
  206.2 1.3 fusion.57
  207.6 2.7 scatter_fusion
  210.3 1.3 fusion.56
  211.6 1.3 fusion.57
  213.0 2.6 scatter_fusion
  215.7 1.3 fusion.56
  216.9 1.3 fusion.57
  218.4 2.6 scatter_fusion
  221.1 1.2 fusion.56
  222.3 1.3 fusion.57
  223.8 2.7 scatter_fusion
  226.4 1.3 fusion.56
  227.7 1.3 fusion.57
  229.1 2.6 scatter_fusion
  231.8 1.2 fusion.56
  233.0 1.3 fusion.57
  234.5 2.6 scatter_fusion
  237.1 1.2 fusion.56
  238.4 1.3 fusion.57
  239.8 2.7 scatter_fusion
  242.5 1.3 fusion.56
  243.8 1.3 fusion.57
  245.2 2.7 scatter_fusion
  249.1 1.3 fusion.57
  250.6 2.7 scatter_fusion
  253.3 3.9 %copy_bitcast_fusion = bf16[128,8192]{1,0:T(8,128)(2,1)} fusion(f32[128,64,128]{2,0,1:T(8,128)} %get-tuple-element.129), kind=kLoop, calls=%fused_computation.25 | loop fusion | flops 1048576 | bytes 6291456 | tf_op jit(solution)/shard_map/convert_element_type | solution.py:55
  258.6 37.0 %all-reduce.5.cloned.1.call-done = (bf16[7,16,128,128]{3,2,1,0:T(8,128)(2,1)}, bf16[7,16,128,128]{3,2,1,0:T(8,128)(2,1)}) async-done(((bf16[7,16,128,128]{3,2,1,0:T(8,128)(2,1)}, bf16[7,16,128,128]{3,2,1,0:T(8,128)(2,1)}), (bf16[7,16,128,128]{3,2,1,0:T(8,128)(2,1)}, bf16[7,16,128,128]{3,2,1,0:T(8,128)(2,1)})) %all-reduce.5.cloned.1.call-update) | async-done | bytes 7340048
  295.6 2.5 constant_dynamic-slice_fusion.1
  298.0 78.4 %reduce-scatter.8.cloned.1.call-done = bf16[128,512]{1,0:T(8,128)(2,1)} async-done(((bf16[128,8192]{1,0:T(8,128)(2,1)}), bf16[128,512]{1,0:T(8,128)(2,1)}) %reduce-scatter.8.cloned.1.call-update) | async-done | bytes 131088 | tf_op jit(solution)/shard_map/reduce_scatter | solution.py:54
  (57 shorter events, 12.4 us)
Async XLA Ops:
  7.2 54.6 %all-gather.4.cloned.1.call-start = ((), (), s32[]{:S(2)}) async-start(), calls=%async_computation.1 | async-start | bytes 2228224 | tf_op jit(solution)/shard_map/all_gather | solution.py:16
  8.9 98.2 %all-gather.8.cloned.1.call-start = ((), (), s32[]{:S(2)}) async-start(), calls=%async_computation.3 | async-start | bytes 3899392 | tf_op jit(solution)/shard_map/all_gather | solution.py:25
  10.7 139.1 %all-gather.6.cloned.1.call-start = ((), (), s32[]{:S(2)}) async-start(), calls=%async_computation.2 | async-start | bytes 3899392 | tf_op jit(solution)/shard_map/all_gather | solution.py:24
  12.6 283.0 %all-reduce.5.cloned.1.call-start = ((), (), s32[]{:S(2)}) async-start(), calls=%async_computation.5 | async-start | bytes 14680064
  164.8 211.6 %reduce-scatter.8.cloned.1.call-start = ((), (), s32[]{:S(2)}) async-start(), calls=%async_computation.4 | async-start | bytes 2228224 | tf_op jit(solution)/shard_map/reduce_scatter | solution.py:54
  253.3 3.9 %copy-start = (u32[256]{0:T(256)S(1)}, u32[256]{0:T(256)}, u32[]{:S(2)}) copy-start(u32[256]{0:T(256)} %constant.58) | copy-start | bytes 3076
Sparse Core Ops, SparseCore 0:
  11.0 50.7 all-gather.3
  64.2 42.8 all-gather.7
  109.5 40.2 all-gather.5
  165.0 130.5 all-reduce.4
  299.5 76.8 reduce-scatter.7
where the time goes:
time: 387 us; the launch traced here: 383 us
  waiting for transfers between devices  233 us (60%)
  matrix products  59.2 us (15%)
  other arithmetic  47.8 us (12%)
  local copies, waits for them, and re-layouts  29.3 us (8%)
  between operations  13.8 us (4%)
    reduce_scatter x1, waiting for transfers between devices, shards(): lax.psum_scatter(partial_inputs.reshape(tokens_here, row_blocks * block_s...  78.4 us
    all_gather x1, waiting for transfers between devices, shards(): full_inputs = lax.all_gather(inputs, 'wide', axis=1, tiled=True)  45.8 us
    scatter-add x16, other arithmetic, one_slot(): return running.at[:, targets].add(contribution)  42.4 us
    all_gather x1, waiting for transfers between devices, shards(): lax.all_gather(gate_blocks, 'narrow', axis=1, tiled=True)  38.3 us
    unnamed x6, waiting for transfers between devices  37 us
    all_gather x1, waiting for transfers between devices, shards(): lax.all_gather(up_blocks, 'narrow', axis=1, tiled=True)  33.1 us
    dot_general x16, matrix products, one_slot(): jnp.einsum('tjc,jbc->tjb', d_up, up_slot, preferred_element_type=jnp.floa...  20.2 us
    dot_general x16, matrix products, one_slot(): jnp.einsum('tjc,jbc->tjb', d_gate, gate_slot, preferred_element_type=jnp....  20 us
  transfers between devices with their start and end apart: 5, of which 5 were waited for; matrix products, arithmetic and copies ran while one was open for 31% of the time, Pallas kernels for 0%

commit v1 on v0

v1 whole, which is shorter than its diff:
```python
import functools

import jax
import jax.numpy as jnp
from jax import lax
from jax.experimental import pallas as pl
from jax.experimental.pallas import tpu as pltpu
from jax.sharding import PartitionSpec as P


def layer_kernel(pat_ref, x_ref, w_ref, gh_ref, hid_ref, gin_ref, gw_ref, acc_ref):
    columns, slots = pat_ref.shape
    blk = w_ref.shape[-1]
    acc_ref[...] = jnp.zeros_like(acc_ref)

    def one_column(j, carry):
        def fwd(k, sums):
            g, u = sums
            r = pat_ref[j, k]
            xb = x_ref[:, pl.ds(pl.multiple_of(r * blk, blk), blk)]
            g = g + jnp.dot(xb, w_ref[0, j, k], preferred_element_type=jnp.float32)
            u = u + jnp.dot(xb, w_ref[1, j, k], preferred_element_type=jnp.float32)
            return g, u

        zero = jnp.zeros((x_ref.shape[0], blk), jnp.float32)
        g, u = lax.fori_loop(0, slots, fwd, (zero, zero))
        s = jax.nn.sigmoid(g)
        act = g * s
        deriv = s * (1.0 + g * (1.0 - s))
        cols = pl.ds(pl.multiple_of(j * blk, blk), blk)
        hid_ref[:, cols] = (act * u).astype(hid_ref.dtype)
        cot = gh_ref[:, cols].astype(jnp.float32)
        dg = (cot * u * deriv).astype(jnp.bfloat16)
        du = (cot * act).astype(jnp.bfloat16)

        def bwd(k, c):
            r = pat_ref[j, k]
            rows = pl.ds(pl.multiple_of(r * blk, blk), blk)
            xb = x_ref[:, rows]
            nt = (((1,), (1,)), ((), ()))
            contrib = lax.dot_general(dg, w_ref[0, j, k], nt, preferred_element_type=jnp.float32)
            contrib = contrib + lax.dot_general(du, w_ref[1, j, k], nt, preferred_element_type=jnp.float32)
            acc_ref[:, rows] += contrib
            tn = (((0,), (0,)), ((), ()))
            gw_ref[k, 0, j] = lax.dot_general(xb, dg, tn, preferred_element_type=jnp.float32).astype(gw_ref.dtype)
            gw_ref[k, 1, j] = lax.dot_general(xb, du, tn, preferred_element_type=jnp.float32).astype(gw_ref.dtype)
            return c

        lax.fori_loop(0, slots, bwd, 0)
        return carry

    lax.fori_loop(0, columns, one_column, 0)
    gin_ref[...] = acc_ref[...].astype(gin_ref.dtype)


def local_layer(x_full, w_all, pattern, grad_hidden):
    tokens, width = x_full.shape
    _, columns, slots, blk, _ = w_all.shape
    vmem = pl.BlockSpec(memory_space=pltpu.VMEM)
    flops = 2 * tokens * columns * slots * blk * blk * 6
    return pl.pallas_call(
        layer_kernel,
        out_shape=(
            jax.ShapeDtypeStruct((tokens, columns * blk), jnp.bfloat16),
            jax.ShapeDtypeStruct((tokens, width), jnp.bfloat16),
            jax.ShapeDtypeStruct((slots, 2, columns, blk, blk), jnp.bfloat16),
        ),
        in_specs=[pl.BlockSpec(memory_space=pltpu.SMEM), vmem, vmem, vmem],
        out_specs=(vmem, vmem, vmem),
        scratch_shapes=[pltpu.VMEM((tokens, width), jnp.float32)],
        compiler_params=pltpu.CompilerParams(vmem_limit_bytes=60 * 1024 * 1024),
        cost_estimate=pl.CostEstimate(
            flops=flops, transcendentals=tokens * columns * blk,
            bytes_accessed=2 * (x_full.size * 2 + w_all.size * 2)),
    )(pattern, x_full, w_all, grad_hidden)


def shards(inputs, gate_blocks, up_blocks, pattern, grad_hidden):
    x_full = lax.all_gather(inputs, "wide", axis=1, tiled=True)
    w_local = jnp.stack([gate_blocks, up_blocks])
    w_all = lax.all_gather(w_local, "narrow", axis=2, tiled=True)
    hidden, gin_partial, gw_terms = local_layer(x_full, w_all, pattern, grad_hidden)
    grad_inputs = lax.psum_scatter(gin_partial, "wide", scatter_dimension=1, tiled=True)
    gw = lax.psum_scatter(gw_terms, "narrow", scatter_dimension=0, tiled=True)
    grad_gate = gw[:, 0].transpose(1, 0, 2, 3)
    grad_up = gw[:, 1].transpose(1, 0, 2, 3)
    return hidden, grad_inputs, grad_gate, grad_up


def solution(mesh):
    placed = (
        P("narrow", "wide"),
        P("wide", "narrow", None, None),
        P("wide", "narrow", None, None),
        P("wide", None),
        P("narrow", "wide"),
    )
    return jax.shard_map(
        shards,
        mesh=mesh,
        in_specs=placed,
        out_specs=(
            P("narrow", "wide"),
            P("narrow", "wide"),
            P("wide", "narrow", None, None),
            P("wide", "narrow", None, None),
        ),
        check_vma=False,
    )
```

time: 387 us -> 325 us (0.84)
  matrix products: 59.2 us -> 0 us
  Pallas kernels: 0 us -> 50.4 us
  other arithmetic: 47.8 us -> 1.85 us
  local copies, waits for them, and re-layouts: 29.3 us -> 1.85 us
  waiting for transfers between devices: 233 us -> 255 us
    reduce_scatter x1 -> x2, waiting for transfers between devices: 78.4 us -> 145 us  [the longest x1 78.3 us: shards(): lax.psum_scatter(gin_partial, 'wide', scatter_dimension=1, tiled=True)]
    dot_general x36 -> x0, matrix products: 59.2 us -> none  [the longest x16 20.2 us: one_slot(): jnp.einsum('tjc,jbc->tjb', d_up, up_slot, preferred_element_type=jnp.floa...]
    pallas_call x0 -> x1, Pallas kernels: none -> 50.4 us  [local_layer(): pl.pallas_call(layer_kernel, out_shape=(jax.ShapeDtypeStruct((tokens, col...]
    scatter-add x16 -> x0, other arithmetic: 42.4 us -> none  [one_slot(): return running.at[:, targets].add(contribution)]
    unnamed x6 -> x4, waiting for transfers between devices: 37 us -> 1.24 us
    gather x2 -> x0, local copies, waits for them, and re-layouts: 9.05 us -> none  [picks_for(): return jnp.take(input_blocks, pattern, axis=1)]
    all_gather x3 -> x2, waiting for transfers between devices: 117 us -> 108 us  [the longest x1 54.1 us: shards(): w_all = lax.all_gather(w_local, 'narrow', axis=2, tiled=True)]
    unnamed x8 -> x1, local copies, waits for them, and re-layouts: 9.13 us -> 1.85 us
  transfers between devices with their start and end apart: 5 -> 4, of which waited for: 5 -> 4; matrix products, arithmetic and copies ran while one was open for 31% -> 1% of each run, Pallas kernels for 0% -> 0%
where the time goes in v1:
time: 325 us; the launch traced here: 323 us
  waiting for transfers between devices  255 us (78%)
  Pallas kernels  50.4 us (16%)
  between operations  13.8 us (4%)
    reduce_scatter x1, waiting for transfers between devices, shards(): lax.psum_scatter(gin_partial, 'wide', scatter_dimension=1, tiled=True)  78.3 us
    reduce_scatter x1, waiting for transfers between devices, shards(): gw = lax.psum_scatter(gw_terms, 'narrow', scatter_dimension=0, tiled=True)  66.8 us
    all_gather x1, waiting for transfers between devices, shards(): w_all = lax.all_gather(w_local, 'narrow', axis=2, tiled=True)  54.1 us
    all_gather x1, waiting for transfers between devices, shards(): x_full = lax.all_gather(inputs, 'wide', axis=1, tiled=True)  54 us
    pallas_call x1, Pallas kernels, local_layer(): pl.pallas_call(layer_kernel, out_shape=(jax.ShapeDtypeStruct((tokens, col...  50.4 us
  transfers between devices with their start and end apart: 4, of which 4 were waited for; matrix products, arithmetic and copies ran while one was open for 1% of the time, Pallas kernels for 0%

profile of v1, /device:TPU:28, one launch (start us, length us, event | category | flops | bytes accessed | tf_op | source)
XLA Modules:
  0.0 322.6 jit_solution(10060035470625224558)
XLA Ops:
  7.2 0.0 all-gather.3.cloned.1.call-start
  7.2 0.7 all-gather.3.cloned.1.call-update
  7.9 0.0 all-gather.5.cloned.1.call-start
  7.9 1.9 pad_maximum_fusion
  9.8 0.0 all-gather.5.cloned.1.call-update
  9.8 0.0 reduce-scatter.5.cloned.1.call-start
  9.9 54.0 %all-gather.3.cloned.1.call-done.x_ref = bf16[128,8192]{1,0:T(8,128)(2,1)} async-done(((bf16[128,512]{1,0:T(8,128)(2,1)}), bf16[128,8192]{1,0:T(8,128)(2,1)}) %all-gather.3.cloned.1.call-update) | async-done | bytes 2097168 | tf_op jit(solution)/shard_map/all_gather | solution.py:79
  63.9 54.1 %all-gather.5.cloned.1.call-done.w_ref = bf16[2,7,16,128,128]{4,3,2,1,0:T(8,128)(2,1)} async-done(((bf16[2,7,1,128,128]{4,3,2,1,0:T(8,128)(2,1)}), bf16[2,7,16,128,128]{4,3,2,1,0:T(8,128)(2,1)}) %all-gather.5.cloned.1.call-update) | async-done | bytes 7340048 | tf_op jit(solution)/shard_map/all_gather | solution.py:81
  118.1 50.4 %shard_map.84 = (bf16[128,896]{1,0:T(8,128)(2,1)}, bf16[128,8192]{1,0:T(8,128)(2,1)}, bf16[16,2,7,128,128]{4,3,2,1,0:T(8,128)(2,1)}) custom-call(s32[7,16]{1,0:T(8,128)} %pat_ref.1, bf16[128,8192]{1,0:T(8,128)(2,1)} %all-gather.3.cloned.1.call-done.x_ref, bf16[2,7,16,128,128]{4,3,2,1,0:T(8,128)(2,1)} %all-gather.5.cloned.1.call-done.w_ref, ...), custom_call_target="tpu_custom_call" | custom-call | flops 2818572288 | bytes 18874368 | tf_op jit(solution)/shard_map/pallas_call | solution.py:61
  168.5 0.0 reduce-scatter.5.cloned.1.call-update
  168.5 0.0 reduce-scatter.3.cloned.1.call-start
  168.5 0.5 reduce-scatter.3.cloned.1.call-update
  169.1 66.8 %reduce-scatter.5.cloned.1.call-done = bf16[1,2,7,128,128]{4,3,2,1,0:T(8,128)(2,1)} async-done(((bf16[16,2,7,128,128]{4,3,2,1,0:T(8,128)(2,1)}), bf16[1,2,7,128,128]{4,3,2,1,0:T(8,128)(2,1)}) %reduce-scatter.5.cloned.1.call-update) | async-done | bytes 458768 | tf_op jit(solution)/shard_map/reduce_scatter | solution.py:84
  235.9 1.8 slice_bitcast_fusion
  237.8 78.3 %reduce-scatter.3.cloned.1.call-done = bf16[128,512]{1,0:T(8,128)(2,1)} async-done(((bf16[128,8192]{1,0:T(8,128)(2,1)}), bf16[128,512]{1,0:T(8,128)(2,1)}) %reduce-scatter.3.cloned.1.call-update) | async-done | bytes 131088 | tf_op jit(solution)/shard_map/reduce_scatter | solution.py:83
Async XLA Ops:
  7.2 56.7 %all-gather.3.cloned.1.call-start = ((), (), s32[]{:S(2)}) async-start(), calls=%async_computation.2 | async-start | bytes 2228224 | tf_op jit(solution)/shard_map/all_gather | solution.py:79
  7.9 110.2 %all-gather.5.cloned.1.call-start = ((), (), s32[]{:S(2)}) async-start(), calls=%async_computation.3 | async-start | bytes 7798784 | tf_op jit(solution)/shard_map/all_gather | solution.py:81
  9.8 226.1 %reduce-scatter.5.cloned.1.call-start = ((), (), s32[]{:S(2)}) async-start(), calls=%async_computation.5 | async-start | bytes 7798784 | tf_op jit(solution)/shard_map/reduce_scatter | solution.py:84
  168.5 147.5 %reduce-scatter.3.cloned.1.call-start = ((), (), s32[]{:S(2)}) async-start(), calls=%async_computation.4 | async-start | bytes 2228224 | tf_op jit(solution)/shard_map/reduce_scatter | solution.py:83
Sparse Core Ops, SparseCore 0:
  10.4 53.4 all-gather.2
  65.8 52.2 all-gather.4
  168.6 67.2 reduce-scatter.4
  239.9 76.0 reduce-scatter.2
